TPU v7x, 256 devices: a whole 4x4x8 slice. The times are simulated.
256 devices in a mesh: seq: 64 (over y, z, core), grp: 4 (over x).
Axes of the slice: x: 4, y: 4, z: 8, core: 2. Of those that a mesh axis runs over, the one named last changes fastest.
Arguments:
- doc_lengths: int32 [4, 16], P('grp'), may hold values from 1 to 1024, 8192 in all within a row
- hidden: bfloat16 [4, 8192, 7168], P('grp', 'seq'), may hold values from -16 to 16
- gate_weight: bfloat16 [7168, 64], P(('seq', 'grp')), may hold values from -0.0625 to 0.0625
- target_query: bfloat16 [4, 8192, 36864], P('grp', 'seq'), may hold values from -30 to 30
- latent_keys: bfloat16 [4, 8192, 576], P('grp', 'seq'), may hold values from -6 to 6
- index_query: bfloat16 [4, 8192, 8192], P('grp', 'seq'), may hold values from -15 to 15
- index_keys: bfloat16 [4, 8192, 128], P('grp', 'seq'), may hold values from -6 to 6
Outputs:
- divergence: float32 [4, 8192], P('grp', 'seq')
- grad_gate: float32 [7168, 64], P(('seq', 'grp'))
All inputs are finite; a program needn't handle non-finite values.
Results may differ from a plain program's by a relative error of at most 0.0022.
Values may be sent and summed in bfloat16 or wider, within the bound.
A program may use at most 128 MiB of HBM per device.

v0:
```python
import jax
import jax.numpy as jnp
from jax import lax
from jax.sharding import Mesh
from jax.sharding import PartitionSpec as P

LOOK = 8
SEQ = ("seq_0", "seq_1", "seq_2")
SEQ_GRP = ("seq_0", "seq_1", "seq_2", "grp")


target_scale = 0.07216878364870322
highest = lax.Precision.HIGHEST
floor_value = -1e30


def shifted(block, axis, distance):
    devices = range(lax.axis_size(axis))
    route = [(i - distance, i) for i in devices if i - distance in devices]
    return lax.ppermute(block, axis, route)


def reduced_to_own(blocks, axes, sequence):
    inside = blocks.shape[1:]
    blocks = blocks.reshape(*(lax.axis_size(a) for a in axes), *inside)
    blocks = jnp.moveaxis(blocks, sequence, range(len(axes))).reshape(-1, *inside)
    for k in sequence:
        blocks = lax.psum_scatter(blocks, axes[k], scatter_dimension=0, tiled=True)
    return blocks[0]


def split_up(value, dim, peers):
    lengths = value.shape
    blocks = value.reshape(*lengths[:dim], peers, lengths[dim] // peers, *lengths[dim + 1 :])
    return jnp.moveaxis(blocks, dim, 0)


def scatter_axes(value, axes, sequence, dim):
    peers = lax.axis_size(axes)
    return reduced_to_own(split_up(value, dim, peers), axes, sequence)


def piece_terms(
    target_rows,
    index_rows,
    gate_rows,
    latent_panel,
    index_panel,
    panel_start_offset,
    positions,
    lengths,
    doc_most,
):
    piece_count, piece_rows = positions.shape
    latent_width = latent_panel.shape[1]
    index_width = index_panel.shape[1]
    key_tile = 128
    span_keys = (doc_most + piece_rows - 1 + key_tile - 1) // key_tile * key_tile
    doc_ends = jnp.cumsum(lengths)
    starts = jnp.sum(lengths * (doc_ends <= positions[..., None]).astype(jnp.int32), -1)
    tile_counts = (positions[:, -1] + 1 - starts[:, 0] + key_tile - 1) // key_tile
    ranking = jnp.argsort(tile_counts, stable=True)
    batch_pieces = max(1, 16 // piece_rows)
    batch_count = piece_count // batch_pieces
    factor = index_width ** (-0.5)
    latent_padded = jnp.concatenate(
        [latent_panel, jnp.zeros((key_tile, latent_width), latent_panel.dtype)], 0
    )
    index_padded = jnp.concatenate(
        [index_panel, jnp.zeros((key_tile, index_width), index_panel.dtype)], 0
    )
    offsets = jnp.arange(key_tile, dtype=jnp.int32)

    def one_batch(batch_index):
        chosen = lax.dynamic_slice_in_dim(ranking, batch_index * batch_pieces, batch_pieces, 0)
        queries = jnp.take(target_rows, chosen, axis=0).reshape(
            batch_pieces, piece_rows, -1, latent_width
        )
        indexer_query_rows = jnp.take(index_rows, chosen, axis=0).reshape(
            batch_pieces, piece_rows, -1, index_width
        )
        gate_values = jnp.take(gate_rows, chosen, axis=0)
        row_pos = jnp.take(positions, chosen, axis=0)
        row_start = jnp.take(starts, chosen, axis=0)
        anchor = row_start[:, 0]
        turn_count = jnp.max(jnp.take(tile_counts, chosen, axis=0))
        head_count = queries.shape[2]
        gate_heads = gate_values.shape[2]

        def allowed_of(turn_index):
            key_pos = anchor[:, None] + turn_index * key_tile + offsets[None, :]
            return (key_pos[:, None, :] >= row_start[:, :, None]) & (
                key_pos[:, None, :] <= row_pos[:, :, None]
            )

        def cut_panel(first_key):
            return (
                lax.dynamic_slice_in_dim(
                    latent_padded, first_key - panel_start_offset, key_tile, 0
                ),
                lax.dynamic_slice_in_dim(index_padded, first_key - panel_start_offset, key_tile, 0),
            )

        def first_pass(turn_index, carry):
            logit_store, relu_store, head_peak, head_total, score_peak, score_total = carry
            latent_tile, indexer_key_block = jax.vmap(cut_panel)(anchor + turn_index * key_tile)
            allowed = allowed_of(turn_index)
            logits = (
                jnp.einsum(
                    "brhc,bkc->brhk", queries, latent_tile, preferred_element_type=jnp.float32
                )
                * target_scale
            )
            relu_score = jnp.maximum(
                jnp.einsum(
                    "fjme,fve->fjmv",
                    indexer_query_rows,
                    indexer_key_block,
                    preferred_element_type=jnp.float32,
                ),
                0.0,
            )
            score = factor * jnp.einsum("brh,brhk->brk", gate_values, relu_score, precision=highest)
            masked = jnp.where(allowed[:, :, None, :], logits, floor_value)
            new_peak = jnp.maximum(head_peak, jnp.max(masked, -1))
            head_total = head_total * jnp.exp(head_peak - new_peak) + jnp.sum(
                jnp.where(allowed[:, :, None, :], jnp.exp(masked - new_peak[..., None]), 0.0), -1
            )
            masked_score = jnp.where(allowed, score, floor_value)
            new_score_peak = jnp.maximum(score_peak, jnp.max(masked_score, -1))
            score_total = score_total * jnp.exp(score_peak - new_score_peak) + jnp.sum(
                jnp.where(allowed, jnp.exp(masked_score - new_score_peak[..., None]), 0.0), -1
            )
            logit_store = lax.dynamic_update_slice_in_dim(
                logit_store, logits, turn_index * key_tile, 3
            )
            relu_store = lax.dynamic_update_slice_in_dim(
                relu_store, relu_score, turn_index * key_tile, 3
            )
            return (logit_store, relu_store, new_peak, head_total, new_score_peak, score_total)

        start_carry = (
            jnp.zeros((batch_pieces, piece_rows, head_count, span_keys), jnp.float32),
            jnp.zeros((batch_pieces, piece_rows, gate_heads, span_keys), jnp.float32),
            jnp.full((batch_pieces, piece_rows, head_count), floor_value, jnp.float32),
            jnp.zeros((batch_pieces, piece_rows, head_count), jnp.float32),
            jnp.full((batch_pieces, piece_rows), floor_value, jnp.float32),
            jnp.zeros((batch_pieces, piece_rows), jnp.float32),
        )
        logit_store, relu_store, head_peak, head_total, score_peak, score_total = lax.fori_loop(
            0, turn_count, first_pass, start_carry
        )
        head_log = head_peak + jnp.log(head_total)
        score_log = score_peak + jnp.log(score_total)

        def second_pass(turn_index, carry):
            row_div, delta_terms = carry
            allowed = allowed_of(turn_index)
            logits = lax.dynamic_slice_in_dim(logit_store, turn_index * key_tile, key_tile, 3)
            relu_score = lax.dynamic_slice_in_dim(relu_store, turn_index * key_tile, key_tile, 3)
            probabilities = jnp.where(
                allowed[:, :, None, :], jnp.exp(logits - head_log[..., None]), 0.0
            )
            target = jnp.mean(probabilities, axis=2)
            score = factor * jnp.einsum("brh,brhk->brk", gate_values, relu_score, precision=highest)
            log_model = jnp.where(allowed, score - score_log[..., None], 0.0)
            model_prob = jnp.where(allowed, jnp.exp(log_model), 0.0)
            positive = target > 0
            target_log_probabilities = jnp.where(
                positive, target * jnp.log(jnp.where(positive, target, 1.0)), 0.0
            )
            row_div = row_div + jnp.sum(
                jnp.where(allowed, target_log_probabilities - target * log_model, 0.0), -1
            )
            delta_terms = delta_terms + factor * jnp.einsum(
                "brk,brhk->brh", model_prob - target, relu_score, precision=highest
            )
            return (row_div, delta_terms)

        return lax.fori_loop(
            0,
            turn_count,
            second_pass,
            (
                jnp.zeros((batch_pieces, piece_rows), jnp.float32),
                jnp.zeros((batch_pieces, piece_rows, gate_heads), jnp.float32),
            ),
        )

    sorted_div, sorted_delta = lax.map(one_batch, jnp.arange(batch_count, dtype=jnp.int32))
    sorted_div = sorted_div.reshape(piece_count, piece_rows)
    sorted_delta = sorted_delta.reshape(piece_count, piece_rows, -1)
    row_div = jnp.zeros_like(sorted_div).at[ranking].set(sorted_div)
    delta_terms = jnp.zeros_like(sorted_delta).at[ranking].set(sorted_delta)
    return (row_div, delta_terms)


def body(doc_lengths, hidden, gate_weight, target_query, latent_keys, index_query, index_keys):
    seq_count = lax.axis_size(SEQ)
    my_index = lax.axis_index(SEQ)
    row_count = hidden.shape[1]
    reach_devices = min(LOOK, seq_count // 2)
    doc_most = reach_devices * row_count
    lengths = doc_lengths[0]
    full_gate = lax.all_gather(gate_weight, SEQ_GRP, axis=0, tiled=True)
    block_rows = 16
    block_count = row_count // block_rows
    latent_parts = []
    index_parts = []
    for offset in range(reach_devices, 0, -1):
        latent_prev, index_prev = shifted((latent_keys[0], index_keys[0]), SEQ, offset)
        latent_parts.append(latent_prev)
        index_parts.append(index_prev)
    latent_win = jnp.concatenate(latent_parts + [latent_keys[0]], 0)
    index_win = jnp.concatenate(index_parts + [index_keys[0]], 0)
    panel_start_offset = my_index * row_count - doc_most
    positions = (my_index * row_count + jnp.arange(row_count, dtype=jnp.int32)).reshape(
        block_count, block_rows
    )
    gates_home = jnp.dot(hidden[0], full_gate, preferred_element_type=jnp.float32).reshape(
        block_count, block_rows, -1
    )
    row_div, delta_terms = piece_terms(
        target_query[0].reshape(block_count, block_rows, -1),
        index_query[0].reshape(block_count, block_rows, -1),
        gates_home,
        latent_win,
        index_win,
        panel_start_offset,
        positions,
        lengths,
        doc_most,
    )
    gate_delta = (delta_terms.reshape(row_count, -1) / row_count).astype(jnp.bfloat16)
    partial_value = jnp.dot(hidden[0].T, gate_delta, preferred_element_type=jnp.float32)
    divergence = row_div.reshape(1, row_count)
    grad_gate = scatter_axes(partial_value, SEQ_GRP, (2, 0, 1, 3), 0)
    return (divergence, grad_gate)


def solution(mesh):
    split = Mesh(
        mesh.devices.reshape(4, 8, 2, mesh.shape["grp"]), ("seq_0", "seq_1", "seq_2", "grp")
    )
    in_specs = (
        P("grp", None),
        P("grp", SEQ, None),
        P(SEQ_GRP, None),
        P("grp", SEQ, None),
        P("grp", SEQ, None),
        P("grp", SEQ, None),
        P("grp", SEQ, None),
    )
    out_specs = (P("grp", SEQ), P(SEQ_GRP, None))
    return jax.shard_map(body, mesh=split, in_specs=in_specs, out_specs=out_specs, check_vma=False)
```

profile of v0, /device:TPU:8, one launch (start us, length us, event | category | flops | bytes accessed | tf_op | source)
XLA Modules:
  0.0 1291.1 jit_solution(13120426017892355332)
XLA Ops:
  7.2 9.2 collective-permute-start
  34.3 134.9 %all-gather = bf16[256,28,64]{2,1,0:T(8,128)(2,1)} all-gather(bf16[1,28,64]{2,1,0:T(8,128)(2,1)} %bitcast.295), channel_id=1, replica_groups=mesh['seq_0'=4,'seq_1'=8,'seq_2'=2,'grp'=4] {'seq_0','seq_1','seq_2','grp'}, dimensions={0}, use_global_device_ids=true | all-gather | bytes 921088 | tf_op jit(solution)/shard_map/all_gather | solution.py:205
  188.7 7.8 collective-permute-done.10
  257.5 499.9 %while.59 = (s32[]{:T(128)}, f32[8,1,16]{2,1,0:T(1,128)S(1)}, f32[8,1,16,64]{3,2,1,0:T(8,128)}, s32[8]{0:T(128)S(1)}, s32[8]{0:T(128)S(1)}, /*index=5*/s32[8]{0:...) while((s32[]{:T(128)}, f32[8,1,16]{2,1,0:T(1,128)S(1)}, ...), condition=%wide.region_14.16_spmd.clone.clone, body=%wide.region_3.15_spmd.clone.clone.sunk | while | flops 191511280 | bytes 22292232 | solution.py:190
  275.6 18.3 %while.60 = (s32[]{:T(128)}, f32[1,16,64,1152]{3,2,1,0:T(8,128)}, f32[1,16,64,1152]{3,2,1,0:T(8,128)}, f32[1,16,64]{2,1,0:T(8,128)S(1)}, f32[1,16,64]{2,1,0:T(8,...) while((s32[]{:T(128)}, f32[1,16,64,1152]{3,2,1,0:T(8,128)}, ...), condition=%wide.region_9.10_spmd, body=%wide.region_4.9_spmd.sunk | while | flops 187207856 | bytes 5385245 | solution.py:150
  293.9 15.6 %while.61 = (s32[]{:T(128)}, f32[1,16]{1,0:T(1,128)S(1)}, f32[1,16,64]{2,1,0:T(8,128)S(1)}, s32[]{:T(128)}, s32[1,1]{1,0:T(1,128)S(1)}, /*index=5*/s32[128]{0:T(...) while((s32[]{:T(128)}, f32[1,16]{1,0:T(1,128)S(1)}, ...), condition=%wide.region_13.14_spmd, body=%wide.region_10.13_spmd.sunk | while | flops 3580039 | bytes 1653543 | solution.py:180
  328.2 24.4 %while.60 = (s32[]{:T(128)}, f32[1,16,64,1152]{3,2,1,0:T(8,128)}, f32[1,16,64,1152]{3,2,1,0:T(8,128)}, f32[1,16,64]{2,1,0:T(8,128)S(1)}, f32[1,16,64]{2,1,0:T(8,...) while((s32[]{:T(128)}, f32[1,16,64,1152]{3,2,1,0:T(8,128)}, ...), condition=%wide.region_9.10_spmd, body=%wide.region_4.9_spmd.sunk | while | flops 187207856 | bytes 5385245 | solution.py:150
  352.6 20.8 %while.61 = (s32[]{:T(128)}, f32[1,16]{1,0:T(1,128)S(1)}, f32[1,16,64]{2,1,0:T(8,128)S(1)}, s32[]{:T(128)}, s32[1,1]{1,0:T(1,128)S(1)}, /*index=5*/s32[128]{0:T(...) while((s32[]{:T(128)}, f32[1,16]{1,0:T(1,128)S(1)}, ...), condition=%wide.region_13.14_spmd, body=%wide.region_10.13_spmd.sunk | while | flops 3580039 | bytes 1653543 | solution.py:180
  392.1 24.3 %while.60 = (s32[]{:T(128)}, f32[1,16,64,1152]{3,2,1,0:T(8,128)}, f32[1,16,64,1152]{3,2,1,0:T(8,128)}, f32[1,16,64]{2,1,0:T(8,128)S(1)}, f32[1,16,64]{2,1,0:T(8,...) while((s32[]{:T(128)}, f32[1,16,64,1152]{3,2,1,0:T(8,128)}, ...), condition=%wide.region_9.10_spmd, body=%wide.region_4.9_spmd.sunk | while | flops 187207856 | bytes 5385245 | solution.py:150
  416.5 20.8 %while.61 = (s32[]{:T(128)}, f32[1,16]{1,0:T(1,128)S(1)}, f32[1,16,64]{2,1,0:T(8,128)S(1)}, s32[]{:T(128)}, s32[1,1]{1,0:T(1,128)S(1)}, /*index=5*/s32[128]{0:T(...) while((s32[]{:T(128)}, f32[1,16]{1,0:T(1,128)S(1)}, ...), condition=%wide.region_13.14_spmd, body=%wide.region_10.13_spmd.sunk | while | flops 3580039 | bytes 1653543 | solution.py:180
  456.0 24.3 %while.60 = (s32[]{:T(128)}, f32[1,16,64,1152]{3,2,1,0:T(8,128)}, f32[1,16,64,1152]{3,2,1,0:T(8,128)}, f32[1,16,64]{2,1,0:T(8,128)S(1)}, f32[1,16,64]{2,1,0:T(8,...) while((s32[]{:T(128)}, f32[1,16,64,1152]{3,2,1,0:T(8,128)}, ...), condition=%wide.region_9.10_spmd, body=%wide.region_4.9_spmd.sunk | while | flops 187207856 | bytes 5385245 | solution.py:150
  480.4 20.8 %while.61 = (s32[]{:T(128)}, f32[1,16]{1,0:T(1,128)S(1)}, f32[1,16,64]{2,1,0:T(8,128)S(1)}, s32[]{:T(128)}, s32[1,1]{1,0:T(1,128)S(1)}, /*index=5*/s32[128]{0:T(...) while((s32[]{:T(128)}, f32[1,16]{1,0:T(1,128)S(1)}, ...), condition=%wide.region_13.14_spmd, body=%wide.region_10.13_spmd.sunk | while | flops 3580039 | bytes 1653543 | solution.py:180
  519.9 24.3 %while.60 = (s32[]{:T(128)}, f32[1,16,64,1152]{3,2,1,0:T(8,128)}, f32[1,16,64,1152]{3,2,1,0:T(8,128)}, f32[1,16,64]{2,1,0:T(8,128)S(1)}, f32[1,16,64]{2,1,0:T(8,...) while((s32[]{:T(128)}, f32[1,16,64,1152]{3,2,1,0:T(8,128)}, ...), condition=%wide.region_9.10_spmd, body=%wide.region_4.9_spmd.sunk | while | flops 187207856 | bytes 5385245 | solution.py:150
  544.3 20.8 %while.61 = (s32[]{:T(128)}, f32[1,16]{1,0:T(1,128)S(1)}, f32[1,16,64]{2,1,0:T(8,128)S(1)}, s32[]{:T(128)}, s32[1,1]{1,0:T(1,128)S(1)}, /*index=5*/s32[128]{0:T(...) while((s32[]{:T(128)}, f32[1,16]{1,0:T(1,128)S(1)}, ...), condition=%wide.region_13.14_spmd, body=%wide.region_10.13_spmd.sunk | while | flops 3580039 | bytes 1653543 | solution.py:180
  583.8 24.3 %while.60 = (s32[]{:T(128)}, f32[1,16,64,1152]{3,2,1,0:T(8,128)}, f32[1,16,64,1152]{3,2,1,0:T(8,128)}, f32[1,16,64]{2,1,0:T(8,128)S(1)}, f32[1,16,64]{2,1,0:T(8,...) while((s32[]{:T(128)}, f32[1,16,64,1152]{3,2,1,0:T(8,128)}, ...), condition=%wide.region_9.10_spmd, body=%wide.region_4.9_spmd.sunk | while | flops 187207856 | bytes 5385245 | solution.py:150
  608.2 20.8 %while.61 = (s32[]{:T(128)}, f32[1,16]{1,0:T(1,128)S(1)}, f32[1,16,64]{2,1,0:T(8,128)S(1)}, s32[]{:T(128)}, s32[1,1]{1,0:T(1,128)S(1)}, /*index=5*/s32[128]{0:T(...) while((s32[]{:T(128)}, f32[1,16]{1,0:T(1,128)S(1)}, ...), condition=%wide.region_13.14_spmd, body=%wide.region_10.13_spmd.sunk | while | flops 3580039 | bytes 1653543 | solution.py:180
  647.7 24.4 %while.60 = (s32[]{:T(128)}, f32[1,16,64,1152]{3,2,1,0:T(8,128)}, f32[1,16,64,1152]{3,2,1,0:T(8,128)}, f32[1,16,64]{2,1,0:T(8,128)S(1)}, f32[1,16,64]{2,1,0:T(8,...) while((s32[]{:T(128)}, f32[1,16,64,1152]{3,2,1,0:T(8,128)}, ...), condition=%wide.region_9.10_spmd, body=%wide.region_4.9_spmd.sunk | while | flops 187207856 | bytes 5385245 | solution.py:150
  672.1 20.8 %while.61 = (s32[]{:T(128)}, f32[1,16]{1,0:T(1,128)S(1)}, f32[1,16,64]{2,1,0:T(8,128)S(1)}, s32[]{:T(128)}, s32[1,1]{1,0:T(1,128)S(1)}, /*index=5*/s32[128]{0:T(...) while((s32[]{:T(128)}, f32[1,16]{1,0:T(1,128)S(1)}, ...), condition=%wide.region_13.14_spmd, body=%wide.region_10.13_spmd.sunk | while | flops 3580039 | bytes 1653543 | solution.py:180
  711.6 24.3 %while.60 = (s32[]{:T(128)}, f32[1,16,64,1152]{3,2,1,0:T(8,128)}, f32[1,16,64,1152]{3,2,1,0:T(8,128)}, f32[1,16,64]{2,1,0:T(8,128)S(1)}, f32[1,16,64]{2,1,0:T(8,...) while((s32[]{:T(128)}, f32[1,16,64,1152]{3,2,1,0:T(8,128)}, ...), condition=%wide.region_9.10_spmd, body=%wide.region_4.9_spmd.sunk | while | flops 187207856 | bytes 5385245 | solution.py:150
  736.0 20.8 %while.61 = (s32[]{:T(128)}, f32[1,16]{1,0:T(1,128)S(1)}, f32[1,16,64]{2,1,0:T(8,128)S(1)}, s32[]{:T(128)}, s32[1,1]{1,0:T(1,128)S(1)}, /*index=5*/s32[128]{0:T(...) while((s32[]{:T(128)}, f32[1,16]{1,0:T(1,128)S(1)}, ...), condition=%wide.region_13.14_spmd, body=%wide.region_10.13_spmd.sunk | while | flops 3580039 | bytes 1653543 | solution.py:180
  775.2 380.0 %reduce-scatter.5.cloned.1.call-done = f32[128,28,64]{2,0,1:T(8,128)} async-done(((f32[256,28,64]{2,0,1:T(8,128)}), f32[128,28,64]{2,0,1:T(8,128)}) %reduce-scatter.5.cloned.1.call-update) | async-done | bytes 917520 | tf_op jit(solution)/shard_map/reduce_scatter | solution.py:28
  1155.2 32.7 %reduce-scatter.7.cloned.1.call-done = f32[32,28,64]{2,0,1:T(8,128)} async-done(((f32[128,28,64]{2,0,1:T(8,128)}), f32[32,28,64]{2,0,1:T(8,128)}) %reduce-scatter.7.cloned.1.call-update) | async-done | bytes 229392 | tf_op jit(solution)/shard_map/reduce_scatter | solution.py:28
  1191.0 73.9 %all-reduce.4.cloned.1.call-done = f32[32,28,64]{2,0,1:T(8,128)} async-done(((f32[32,28,64]{2,0,1:T(8,128)}), f32[32,28,64]{2,0,1:T(8,128)}) %all-reduce.4.cloned.1.call-update) | async-done | bytes 229392
  1265.8 17.5 %all-reduce.1 = f32[4,28,64]{2,0,1:T(4,128)S(1)} all-reduce(f32[4,28,64]{2,0,1:T(4,128)S(1)} %constant_dynamic-slice_fusion.3), channel_id=5, replica_groups=mesh['seq_0'=4,'seq_1'=8,'seq_2'=2,'grp'=4] {'grp'}, use_global_device_ids=true, to_apply=%region_20.22.clone | all-reduce | flops 7168 | bytes 57344
  (996 shorter events, 574.3 us)
Async XLA Ops:
  7.2 167.0 %copy-start = (bf16[1,128,7168]{2,1,0:T(8,128)(2,1)S(1)}, bf16[1,128,7168]{2,1,0:T(8,128)(2,1)}, u32[]{:S(2)}) copy-start(bf16[1,128,7168]{2,1,0:T(8,128)(2,1)} %param.16) | copy-start | bytes 5505028
  7.2 1148.0 %reduce-scatter.5.cloned.1.call-start = ((), (), s32[]{:S(2)}) async-start(), calls=%async_computation.2 | async-start | bytes 5505024 | tf_op jit(solution)/shard_map/reduce_scatter | solution.py:28
  7.2 232.6 %collective-permute-start = (bf16[128,576]{0,1:T(8,128)(2,1)}, bf16[128,576]{0,1:T(8,128)(2,1)S(1)}, u32[]{:S(2)}, u32[]{:S(2)}) collective-permute-start(bf16[128,576]{0,1:T(8,128)(2,1)} %bitcast.276), channel_id=1, source_target_pairs={{0,32},{4,36},{8,40},{12,44},{16,48},{20,52},{24,56},{28,60},{32,6... | collective-permute-start | bytes 442376 | tf_op jit(solution)/shard_map/ppermute | solution.py:20
  16.5 226.1 %collective-permute-start.1 = (bf16[128,576]{0,1:T(8,128)(2,1)}, bf16[128,576]{0,1:T(8,128)(2,1)S(1)}, u32[]{:S(2)}, u32[]{:S(2)}) collective-permute-start(bf16[128,576]{0,1:T(8,128)(2,1)} %bitcast.277), channel_id=1, source_target_pairs={{0,28},{4,32},{8,36},{12,40},{16,44},{20,48},{24,52},{28,56},{32,6... | collective-permute-start | bytes 442376 | tf_op jit(solution)/shard_map/ppermute | solution.py:20
  19.5 225.0 %collective-permute-start.2 = (bf16[128,576]{0,1:T(8,128)(2,1)}, bf16[128,576]{0,1:T(8,128)(2,1)S(1)}, u32[]{:S(2)}, u32[]{:S(2)}) collective-permute-start(bf16[128,576]{0,1:T(8,128)(2,1)} %bitcast.278), channel_id=1, source_target_pairs={{0,24},{4,28},{8,32},{12,36},{16,40},{20,44},{24,48},{28,52},{32,5... | collective-permute-start | bytes 442376 | tf_op jit(solution)/shard_map/ppermute | solution.py:20
  22.5 224.2 %collective-permute-start.3 = (bf16[128,576]{0,1:T(8,128)(2,1)}, bf16[128,576]{0,1:T(8,128)(2,1)S(1)}, u32[]{:S(2)}, u32[]{:S(2)}) collective-permute-start(bf16[128,576]{0,1:T(8,128)(2,1)} %bitcast.279), channel_id=1, source_target_pairs={{0,20},{4,24},{8,28},{12,32},{16,36},{20,40},{24,44},{28,48},{32,5... | collective-permute-start | bytes 442376 | tf_op jit(solution)/shard_map/ppermute | solution.py:20
  29.6 146.8 %collective-permute-start.8 = (bf16[128,128]{1,0:T(8,128)(2,1)}, bf16[128,128]{1,0:T(8,128)(2,1)S(1)}, u32[]{:S(2)}, u32[]{:S(2)}) collective-permute-start(bf16[128,128]{1,0:T(8,128)(2,1)} %bitcast.286), channel_id=1, source_target_pairs={{0,32},{4,36},{8,40},{12,44},{16,48},{20,52},{24,56},{28,60},{32,6... | collective-permute-start | bytes 98312 | tf_op jit(solution)/shard_map/ppermute | solution.py:20
  174.2 2.2 copy-start.4
  174.2 63.7 %copy-start.3 = (bf16[1,128,576]{1,2,0:T(8,128)(2,1)S(1)}, bf16[1,128,576]{1,2,0:T(8,128)(2,1)}, u32[]{:S(2)}) copy-start(bf16[1,128,576]{1,2,0:T(8,128)(2,1)} %param.19) | copy-start | bytes 442372
  176.4 10.3 collective-permute-start.9
  186.8 9.7 collective-permute-start.10
  196.5 9.1 collective-permute-start.11
  205.6 8.8 collective-permute-start.12
  214.4 8.2 collective-permute-start.13
  222.6 7.9 collective-permute-start.14
  230.5 7.3 collective-permute-start.15
  237.9 12.6 collective-permute-start.4
  240.6 12.0 collective-permute-start.5
  242.5 12.4 collective-permute-start.6
  244.5 11.7 collective-permute-start.7
  775.1 412.9 %copy-start.6 = (u32[256]{0:T(256)S(1)}, u32[256]{0:T(256)}, u32[]{:S(2)}) copy-start(u32[256]{0:T(256)} %constant.381) | copy-start | bytes 3076
  775.1 413.5 %copy-start.5 = (u32[256]{0:T(256)S(1)}, u32[256]{0:T(256)}, u32[]{:S(2)}) copy-start(u32[256]{0:T(256)} %constant.385) | copy-start | bytes 3076
  775.1 412.8 %reduce-scatter.7.cloned.1.call-start = ((), (), s32[]{:S(2)}) async-start(), calls=%async_computation.3 | async-start | bytes 2293760 | tf_op jit(solution)/shard_map/reduce_scatter | solution.py:28
  1155.2 109.7 %all-reduce.4.cloned.1.call-start = ((), (), s32[]{:S(2)}) async-start(), calls=%async_computation.4 | async-start | bytes 917504
  (2 other events, 1.8 us)
Sparse Core Ops, SparseCore 0:
  775.2 379.9 reduce-scatter.4
  1157.7 30.1 reduce-scatter.6
  1190.3 74.5 all-reduce.3
where the time goes:
time: 1320 us; the launch traced here: 1290 us
  waiting for transfers between devices  542 us (41%)
  matrix products  263 us (20%)
  blocking collectives  152 us (12%)
  local copies, waits for them, and re-layouts  112 us (8%)
  other arithmetic  112 us (8%)
  starting transfers between devices  48.1 us (4%)
  loops' own time  46 us (3%)
  between operations  14.9 us (1%)
    reduce_scatter x2, waiting for transfers between devices, reduced_to_own(): blocks = lax.psum_scatter(blocks, axes[k], scatter_dimension=0, tiled=True)  413 us
    all_gather x1, blocking collectives, body(): full_gate = lax.all_gather(gate_weight, SEQ_GRP, axis=0, tiled=True)  135 us
    dot_general x31, matrix products, first_pass(): jnp.einsum('brhc,bkc->brhk', queries, latent_tile, preferred_element_type...  74.1 us
    unnamed x4, waiting for transfers between devices  74 us
    dot_general x31, matrix products, second_pass(): jnp.einsum('brk,brhk->brh', model_prob - target, relu_score, precision=hi...  60.9 us
    dot_general x31, matrix products, first_pass(): jnp.einsum('fjme,fve->fjmv', indexer_query_rows, indexer_key_block, prefe...  57.7 us
    ppermute x16, waiting for transfers between devices, shifted(): return lax.ppermute(block, axis, route)  55.6 us
    dot_general x31, matrix products, second_pass(): jnp.einsum('brh,brhk->brk', gate_values, relu_score, precision=highest)  49.6 us
  transfers between devices with their start and end apart: 19, of which 14 were waited for; matrix products, arithmetic and copies ran while one was open for 1% of the time, Pallas kernels for 0%

commit v1 on v0

v1 whole, which is shorter than its diff:
```python
import functools
import math

import jax
import jax.numpy as jnp
from jax import lax
from jax.experimental import pallas as pl
from jax.experimental.pallas import tpu as pltpu
from jax.sharding import Mesh
from jax.sharding import PartitionSpec as P

SEQ = ("seq_0", "seq_1", "seq_2")
SEQ_GRP = ("seq_0", "seq_1", "seq_2", "grp")
MESH = pl.DeviceIdType.MESH

ROWS = 128
HEADS = 64
LAT = 576
DI = 128
WIN = 1152
LOOK = 1024
D = 7168
DOCS = 16
PAIR = 2 * LAT
CUT = 640
DEEP = 768
UNIT = 4 * ROWS
SLOTS = 4
NEG = -1e30
TARGET_SCALE = 0.07216878364870322
EXP_SCALE = TARGET_SCALE * math.log2(math.e)
BF = jnp.bfloat16
F32 = jnp.float32
VMEM_MOST = 67_043_328


def compute_kernel(
    lens_ref, q_hbm, iq_hbm, hid_hbm, lat_hbm, ik_hbm, w_hbm,
    div_ref, part_ref,
    ke, ko, ikt, qbuf, rel_a, rel_b, acc, score, dif, gates3, hid, ht, iq, lat, ik, wf, gd,
    qsem, isem,
):
    seq = (lax.axis_index("seq_0") * 8 + lax.axis_index("seq_1")) * 2 + lax.axis_index("seq_2")
    first = lax.axis_index("seq_2") * ROWS

    def q_copy(unit, slot):
        quad, parity = unit // 2, unit % 2
        return [
            pltpu.make_async_copy(
                q_hbm.at[:, pl.ds(pl.multiple_of((quad * 4 + k) * PAIR + parity * (PAIR - CUT), 128), CUT)],
                qbuf.at[slot, pl.ds(k * ROWS, ROWS), pl.ds(0, CUT)],
                qsem.at[slot, k],
            )
            for k in range(4)
        ]

    lat_in = pltpu.make_async_copy(lat_hbm, lat, isem.at[0])
    ik_in = pltpu.make_async_copy(ik_hbm, ik, isem.at[1])
    lat_in.start()
    ik_in.start()
    for s in range(SLOTS):
        for c in q_copy(s, s):
            c.start()
    iq_in = pltpu.make_async_copy(iq_hbm, iq, isem.at[2])
    hid_in = pltpu.make_async_copy(hid_hbm, hid, isem.at[3])
    w_in = pltpu.make_async_copy(w_hbm, wf, isem.at[4])
    iq_in.start()
    hid_in.start()
    w_in.start()

    row = lax.broadcasted_iota(jnp.int32, (ROWS, ROWS), 0)
    lane = lax.broadcasted_iota(jnp.int32, (ROWS, ROWS), 1)
    pos = seq * ROWS + row
    start = jnp.zeros((ROWS, ROWS), jnp.int32)
    end = jnp.int32(0)
    for k in range(DOCS):
        length = lens_ref[0, k]
        end = end + length
        start = start + jnp.where(pos >= end, length, 0)
    eye = jnp.where(row == lane, 1.0, 0.0).astype(BF)
    for s in range(SLOTS):
        for k in range(4):
            qbuf[s, k * ROWS : (k + 1) * ROWS, CUT:DEEP] = eye
    for t in range(WIN // ROWS):
        key = seq * ROWS - LOOK + t * ROWS + lane
        bias = jnp.where(jnp.logical_and(key >= start, key <= pos), 0.0, NEG).astype(BF)
        ke[CUT:DEEP, t * ROWS : (t + 1) * ROWS] = bias
        ko[CUT:DEEP, t * ROWS : (t + 1) * ROWS] = bias
    ke[LAT:CUT, :] = jnp.zeros((CUT - LAT, WIN), BF)
    ko[0 : CUT - LAT, :] = jnp.zeros((CUT - LAT, WIN), BF)
    acc[...] = jnp.zeros((ROWS, WIN), F32)

    lat_in.wait()
    for t in range(WIN // ROWS):
        rows = pl.ds(pl.multiple_of(first + t * ROWS, ROWS), ROWS)
        cols = slice(t * ROWS, (t + 1) * ROWS)
        block = lat[rows, :].T
        ke[0:LAT, cols] = block
        ko[CUT - LAT : CUT, cols] = block
    ik_in.wait()
    for t in range(WIN // ROWS):
        rows = pl.ds(pl.multiple_of(first + t * ROWS, ROWS), ROWS)
        ikt[:, t * ROWS : (t + 1) * ROWS] = ik[rows, :].T

    s_even, s_odd = rel_a.at[0], rel_b.at[0]

    def logits(slot, keys, dest):
        dest[...] = jnp.dot(qbuf[slot], keys[...], preferred_element_type=F32)

    def heads_sum(src):
        for g in range(ROWS // 8):
            rows = slice(8 * g, 8 * g + 8)
            total = acc[rows, :]
            for k in range(4):
                s = src[k * ROWS + 8 * g : k * ROWS + 8 * g + 8, :]
                top = jnp.max(s, axis=1, keepdims=True)
                p = jnp.exp2((s - top) * EXP_SCALE)
                total = total + p * (1.0 / jnp.sum(p, axis=1, keepdims=True))
            acc[rows, :] = total

    def wait_q(unit, slot):
        for c in q_copy(unit, slot):
            c.wait()

    def next_q(unit, slot):
        @pl.when(unit + SLOTS < 16)
        def _():
            for c in q_copy(unit + SLOTS, slot):
                c.start()

    wait_q(0, 0)
    logits(0, ke, s_even)
    next_q(0, 0)

    def pair_step(i, _):
        odd, even = 2 * i + 1, 2 * i + 2
        wait_q(odd, odd % SLOTS)
        logits(odd % SLOTS, ko, s_odd)
        heads_sum(s_even)
        next_q(odd, odd % SLOTS)

        @pl.when(even < 16)
        def _():
            wait_q(even, even % SLOTS)

        logits(even % SLOTS, ke, s_even)
        heads_sum(s_odd)
        next_q(even, even % SLOTS)
        return 0

    lax.fori_loop(0, 8, pair_step, 0)

    hid_in.wait()
    w_in.wait()
    gates = jnp.dot(hid[...], wf[...], preferred_element_type=F32)
    for h in range(HEADS):
        gates3[h] = jnp.broadcast_to(gates[:, h : h + 1], (ROWS, ROWS))
    iq_in.wait()
    score[...] = jnp.zeros((ROWS, WIN), F32)

    def relus(unit, dest):
        q4 = jnp.concatenate(
            [iq[:, pl.ds(pl.multiple_of((unit * 4 + k) * DI, DI), DI)] for k in range(4)], axis=0
        )
        dest[...] = jnp.dot(q4, ikt[...], preferred_element_type=F32)

    def score_sum(unit, src):
        for g in range(ROWS // 8):
            rows = slice(8 * g, 8 * g + 8)
            tiles = [score[rows, t * 128 : t * 128 + 128] for t in range(9)]
            for k in range(4):
                gate = gates3[unit * 4 + k, rows, :]
                for t in range(9):
                    s = src[k * ROWS + 8 * g : k * ROWS + 8 * g + 8, t * 128 : t * 128 + 128]
                    tiles[t] = tiles[t] + gate * jnp.maximum(s, 0.0)
            for t in range(9):
                score[rows, t * 128 : t * 128 + 128] = tiles[t]

    relus(0, rel_a.at[0])

    def score_step(i, _):
        relus(2 * i + 1, rel_b.at[i])
        score_sum(2 * i, rel_a.at[i])
        nxt = jnp.minimum(i + 1, 7)
        relus(2 * nxt, rel_a.at[nxt])
        score_sum(2 * i + 1, rel_b.at[i])
        return 0

    lax.fori_loop(0, 8, score_step, 0)

    factor = DI**-0.5
    for g in range(ROWS // 8):
        rows = slice(8 * g, 8 * g + 8)
        bias = ke[CUT + 16 * (g // 2) : CUT + 16 * (g // 2) + 16, :].astype(F32)[8 * (g % 2) : 8 * (g % 2) + 8, :]
        allowed = bias == 0.0
        sc = jnp.where(allowed, score[rows, :] * factor, NEG)
        shifted = sc - jnp.max(sc, axis=1, keepdims=True)
        log_model = shifted - jnp.log(jnp.sum(jnp.exp(shifted), axis=1, keepdims=True))
        model = jnp.exp(log_model)
        target = acc[rows, :] * (1.0 / HEADS)
        positive = target > 0.0
        terms = jnp.where(positive, target * (jnp.log(jnp.where(positive, target, 1.0)) - log_model), 0.0)
        terms = jnp.where(allowed, terms, 0.0)
        div_ref[rows, :] = jnp.broadcast_to(jnp.sum(terms, axis=1, keepdims=True), (8, 128))
        dif[rows, :] = jnp.where(allowed, model - target, 0.0)

    gd[...] = jnp.zeros((ROWS, ROWS), F32)
    lane8 = lax.broadcasted_iota(jnp.int32, (8, ROWS), 1)

    def delta_sum(unit, src):
        for g in range(ROWS // 8):
            rows = slice(8 * g, 8 * g + 8)
            out = gd[rows, :]
            tiles = [dif[rows, t * 128 : t * 128 + 128] for t in range(9)]
            for k in range(4):
                total = None
                for t in range(9):
                    s = src[k * ROWS + 8 * g : k * ROWS + 8 * g + 8, t * 128 : t * 128 + 128]
                    term = tiles[t] * jnp.maximum(s, 0.0)
                    total = term if total is None else total + term
                value = jnp.sum(total, axis=1, keepdims=True)
                out = jnp.where(lane8 == unit * 4 + k, value, out)
            gd[rows, :] = out

    def delta_step(i, _):
        delta_sum(2 * i, rel_a.at[i])
        delta_sum(2 * i + 1, rel_b.at[i])
        return 0

    for t in range(D // 128):
        ht[t * 128 : t * 128 + 128, :] = hid[:, t * 128 : t * 128 + 128].T
    lax.fori_loop(0, 8, delta_step, 0)

    delta = (gd[...] * factor / ROWS).astype(BF).astype(F32)
    two = jnp.concatenate([delta, pltpu.roll(delta, 64, 1)], axis=0).astype(BF)

    def part_step(i, _):
        lo = pl.ds(pl.multiple_of(i * 224, 16), 112)
        hi = pl.ds(pl.multiple_of(i * 224 + 112, 16), 112)
        both = jnp.concatenate([ht[lo, :], ht[hi, :]], axis=1)
        out = jnp.dot(both, two, preferred_element_type=F32)
        pad = jnp.zeros((2, 128), F32)
        for x in range(4):
            for half in range(2):
                at = x * 28 + half * 14
                part_ref[half, x, i // 8, i % 8] = jnp.concatenate([out[at : at + 14, :], pad], axis=0)
        return 0

    lax.fori_loop(0, 32, part_step, 0)


def compute(lens, q, iq, hid, lat, ik, w):
    hbm = pl.BlockSpec(memory_space=pl.ANY)
    vmem = pl.BlockSpec(memory_space=pltpu.VMEM)
    return pl.pallas_call(
        compute_kernel,
        out_shape=(
            jax.ShapeDtypeStruct((ROWS, 128), F32),
            jax.ShapeDtypeStruct((2, 4, 4, 8, 16, 128), F32),
        ),
        in_specs=[pl.BlockSpec(memory_space=pltpu.SMEM)] + [hbm] * 6,
        out_specs=(vmem, vmem),
        scratch_shapes=[
            pltpu.VMEM((DEEP, WIN), BF),
            pltpu.VMEM((DEEP, WIN), BF),
            pltpu.VMEM((DI, WIN), BF),
            pltpu.VMEM((SLOTS, UNIT, DEEP), BF),
            pltpu.VMEM((8, UNIT, WIN), F32),
            pltpu.VMEM((8, UNIT, WIN), F32),
            pltpu.VMEM((ROWS, WIN), F32),
            pltpu.VMEM((ROWS, WIN), F32),
            pltpu.VMEM((ROWS, WIN), F32),
            pltpu.VMEM((HEADS, ROWS, ROWS), F32),
            pltpu.VMEM((ROWS, D), BF),
            pltpu.VMEM((D, ROWS), BF),
            pltpu.VMEM((ROWS, HEADS * DI), BF),
            pltpu.VMEM((WIN + ROWS, LAT), BF),
            pltpu.VMEM((WIN + ROWS, DI), BF),
            pltpu.VMEM((D, HEADS), BF),
            pltpu.VMEM((ROWS, ROWS), F32),
            pltpu.SemaphoreType.DMA((SLOTS, 4)),
            pltpu.SemaphoreType.DMA((5,)),
        ],
        compiler_params=pltpu.CompilerParams(vmem_limit_bytes=VMEM_MOST),
        cost_estimate=pl.CostEstimate(flops=20_000_000_000, bytes_accessed=18_000_000, transcendentals=9_400_000),
    )(lens, q, iq, hid, lat, ik, w)


def sync_with(peers):
    barrier = pltpu.get_barrier_semaphore()
    for peer in peers:
        pl.semaphore_signal(barrier, inc=1, device_id=peer, device_id_type=MESH)
    pl.semaphore_wait(barrier, len(peers))


def chip_after(y, z):
    return {"seq_0": lax.rem(y + (z + 1) // 8, 4), "seq_1": lax.rem(z + 1, 8)}


def chip_before(y, z):
    return {"seq_0": lax.rem(y + 3 + (z + 7) // 8, 4), "seq_1": lax.rem(z + 7, 8)}


def fetch_kernel(
    lat_ref, ik_ref, gw_ref, lat_out, ik_out, w_out,
    wx, wcat, wb, ring_s, ring_r, side_s, side_r, w_s, w_r,
):
    y, z, core, x = (lax.axis_index(a) for a in SEQ_GRP)
    ahead, behind = chip_after(y, z), chip_before(y, z)
    partner = {"seq_2": 1 - core}
    xs = [{"grp": lax.rem(x + d, 4)} for d in range(1, 4)]
    ys = [{"seq_0": lax.rem(y + d, 4)} for d in range(1, 4)]
    zs = [{"seq_1": lax.rem(z + d, 8)} for d in range(1, 8)]
    sync_with([partner] + xs + ys + zs + [ahead, behind])

    def remote(src, dst, send, recv, peer):
        return pltpu.make_async_remote_copy(
            src_ref=src, dst_ref=dst, send_sem=send, recv_sem=recv, device_id=peer, device_id_type=MESH
        )

    def slot(k):
        return pl.ds(pl.multiple_of((8 - 2 * k + core) * ROWS, ROWS), ROWS)

    wx[x] = gw_ref[...]
    x_copies = []
    for d in range(1, 4):
        c = remote(gw_ref, wx.at[x], w_s.at[d], w_r.at[d], xs[d - 1])
        c.start()
        x_copies.append(c)

    def ring(k, src_lat, src_ik):
        return [
            remote(src_ik, ik_out.at[slot(k + 1)], ring_s.at[k, 0], ring_r.at[k, 0], ahead),
            remote(src_lat, lat_out.at[slot(k + 1)], ring_s.at[k, 1], ring_r.at[k, 1], ahead),
        ]

    def side(k, src_lat, src_ik):
        return [
            remote(src_ik, ik_out.at[slot(k)], side_s.at[k, 0], side_r.at[k, 0], partner),
            remote(src_lat, lat_out.at[slot(k)], side_s.at[k, 1], side_r.at[k, 1], partner),
        ]

    hop = ring(0, lat_ref, ik_ref)
    for c in hop:
        c.start()
    sides = [side(0, lat_ref, ik_ref)]
    for c in sides[0]:
        c.start()
    lat_out[slot(0), :] = lat_ref[...]
    ik_out[slot(0), :] = ik_ref[...]

    for c in x_copies:
        c.wait()
    for j in range(4):
        wcat[28 * j : 28 * j + 28, :] = wx[j].astype(F32)
    wb[core, y, z] = wcat[...].astype(BF)
    z_copies = []
    for d in range(1, 8):
        c = remote(wb.at[core, y, z], wb.at[core, y, z], w_s.at[3 + d], w_r.at[3 + d], zs[d - 1])
        c.start()
        z_copies.append(c)

    for k in range(1, 5):
        for c in hop:
            c.wait()
        here_lat, here_ik = lat_out.at[slot(k)], ik_out.at[slot(k)]
        if k < 4:
            hop = ring(k, here_lat, here_ik)
            for c in hop:
                c.start()
        sides.append(side(k, here_lat, here_ik))
        for c in sides[-1]:
            c.start()
        if k == 1:
            for c in z_copies:
                c.wait()
            y_copies = []
            for d in range(1, 4):
                c = remote(wb.at[core, y], wb.at[core, y], w_s.at[10 + d], w_r.at[10 + d], ys[d - 1])
                c.start()
                y_copies.append(c)
        if k == 3:
            for c in y_copies:
                c.wait()
            last = remote(wb.at[core], wb.at[core], w_s.at[0], w_r.at[0], partner)
            last.start()
    last.wait()
    for yy in range(4):
        for zz in range(8):
            for cc in range(2):
                at = ((yy * 8 + zz) * 2 + cc) * 112
                w_out[at : at + 112, :] = wb[cc, yy, zz]
    for pair in sides:
        for c in pair:
            c.wait()


def fetch(lat, ik, gw):
    vmem = pl.BlockSpec(memory_space=pltpu.VMEM)
    return pl.pallas_call(
        fetch_kernel,
        out_shape=(
            jax.ShapeDtypeStruct((WIN + ROWS, LAT), BF),
            jax.ShapeDtypeStruct((WIN + ROWS, DI), BF),
            jax.ShapeDtypeStruct((D, HEADS), BF),
        ),
        in_specs=[vmem] * 3,
        out_specs=(vmem,) * 3,
        scratch_shapes=[
            pltpu.VMEM((4, 28, HEADS), BF),
            pltpu.VMEM((112, HEADS), F32),
            pltpu.VMEM((2, 4, 8, 112, HEADS), BF),
            pltpu.SemaphoreType.DMA((4, 2)),
            pltpu.SemaphoreType.DMA((4, 2)),
            pltpu.SemaphoreType.DMA((5, 2)),
            pltpu.SemaphoreType.DMA((5, 2)),
            pltpu.SemaphoreType.DMA((14,)),
            pltpu.SemaphoreType.DMA((14,)),
        ],
        compiler_params=pltpu.CompilerParams(collective_id=0, has_side_effects=True, vmem_limit_bytes=VMEM_MOST),
    )(lat, ik, gw)


def reduce_kernel(part_ref, out_ref, rc, s1, rx, s2, ry, s3, rz, s4, fin, ssem, rsem):
    y, z, core, x = (lax.axis_index(a) for a in SEQ_GRP)
    partner = {"seq_2": 1 - core}
    xs = [{"grp": lax.rem(x + d, 4)} for d in range(1, 4)]
    ys = [{"seq_0": lax.rem(y + d, 4)} for d in range(1, 4)]
    zs = [{"seq_1": lax.rem(z + d, 8)} for d in range(1, 8)]
    sync_with([partner] + xs + ys + zs)

    def remote(src, dst, sem, peer):
        return pltpu.make_async_remote_copy(
            src_ref=src, dst_ref=dst, send_sem=ssem.at[sem], recv_sem=rsem.at[sem],
            device_id=peer, device_id_type=MESH,
        )

    def exchange(copies):
        for c in copies:
            c.start()
        for c in copies:
            c.wait()

    exchange([remote(part_ref.at[1 - core, k], rc.at[k], k, partner) for k in range(4)])
    for k in range(4):
        s1[k] = part_ref[core, k] + rc[k]
    exchange([remote(s1.at[lax.rem(x + d, 4)], rx.at[d - 1], 3 + d, xs[d - 1]) for d in range(1, 4)])
    s2[...] = s1[x] + rx[0] + rx[1] + rx[2]
    exchange([remote(s2.at[lax.rem(y + d, 4)], ry.at[d - 1], 6 + d, ys[d - 1]) for d in range(1, 4)])
    s3[...] = s2[y] + ry[0] + ry[1] + ry[2]
    exchange([remote(s3.at[lax.rem(z + d, 8)], rz.at[d - 1], 9 + d, zs[d - 1]) for d in range(1, 8)])
    total = s3[z]
    for d in range(7):
        total = total + rz[d]
    s4[...] = total
    exchange([remote(s4, fin, 17, partner)])
    low = jnp.where(core == 0, s4[...], fin[...])
    high = jnp.where(core == 0, fin[...], s4[...])
    full = jnp.concatenate([low[0:14, :], high[0:14, :]], axis=0)
    out_ref[...] = jnp.where(core == 0, full[:, 0:64], full[:, 64:128])


def reduce_all(part):
    vmem = pl.BlockSpec(memory_space=pltpu.VMEM)
    return pl.pallas_call(
        reduce_kernel,
        out_shape=jax.ShapeDtypeStruct((28, HEADS), F32),
        in_specs=[vmem],
        out_specs=vmem,
        scratch_shapes=[
            pltpu.VMEM((4, 4, 8, 16, 128), F32),
            pltpu.VMEM((4, 4, 8, 16, 128), F32),
            pltpu.VMEM((3, 4, 8, 16, 128), F32),
            pltpu.VMEM((4, 8, 16, 128), F32),
            pltpu.VMEM((3, 8, 16, 128), F32),
            pltpu.VMEM((8, 16, 128), F32),
            pltpu.VMEM((7, 16, 128), F32),
            pltpu.VMEM((16, 128), F32),
            pltpu.VMEM((16, 128), F32),
            pltpu.SemaphoreType.DMA((18,)),
            pltpu.SemaphoreType.DMA((18,)),
        ],
        compiler_params=pltpu.CompilerParams(collective_id=1, has_side_effects=True),
    )(part)


def body(doc_lengths, hidden, gate_weight, target_query, latent_keys, index_query, index_keys):
    lat, ik, w = fetch(latent_keys[0], index_keys[0], gate_weight)
    div, part = compute(doc_lengths, target_query[0], index_query[0], hidden[0], lat, ik, w)
    return div[:, 0].reshape(1, ROWS), reduce_all(part)


def solution(mesh):
    split = Mesh(mesh.devices.reshape(4, 8, 2, mesh.shape["grp"]), SEQ_GRP)
    rows = P("grp", SEQ, None)
    in_specs = (P("grp", None), rows, P(SEQ_GRP, None), rows, rows, rows, rows)
    out_specs = (P("grp", SEQ), P(SEQ_GRP, None))
    return jax.shard_map(body, mesh=split, in_specs=in_specs, out_specs=out_specs, check_vma=False)
```

time: 1320 us -> 139 us (0.11)
  the two profiles are of different devices: /device:TPU:8 before, /device:TPU:1 now
where the time goes in v1:
time: 139 us
  Pallas kernels  134 us (96%)
  local copies, waits for them, and re-layouts  4.49 us (3%)
    pallas_call x1, Pallas kernels, compute(): pl.pallas_call(compute_kernel, out_shape=(jax.ShapeDtypeStruct((ROWS, 128...  51 us
    pallas_call x1, Pallas kernels, fetch(): pl.pallas_call(fetch_kernel, out_shape=(jax.ShapeDtypeStruct((WIN + ROWS,...  49 us
    pallas_call x1, Pallas kernels, reduce_all(): pl.pallas_call(reduce_kernel, out_shape=jax.ShapeDtypeStruct((28, HEADS),...  34 us
    unnamed x2, local copies, waits for them, and re-layouts  3.02 us

profile of v1, /device:TPU:1, one launch (start us, length us, event | category | flops | bytes accessed | tf_op | source)
XLA Modules:
  0.0 139.1 jit_solution(456139827467526316)
XLA Ops:
  0.6 1.7 %copy.10 = bf16[1,128,576]{2,1,0:T(8,128)(2,1)} copy(bf16[1,128,576]{1,2,0:T(8,128)(2,1)} %param.11) | data formatting | bytes 294912 | tf_op args[4]
  2.3 49.0 %shard_map.86 = (bf16[1280,576]{1,0:T(8,128)(2,1)}, bf16[1280,128]{1,0:T(8,128)(2,1)}, bf16[7168,64]{1,0:T(8,128)(2,1)}) custom-call(bf16[128,576]{1,0:T(8,128)(2,1)} %bitcast.6, bf16[128,128]{1,0:T(8,128)(2,1)} %bitcast.7, bf16[28,64]{1,0:T(8,128)(2,1)} %gw_ref.1), custom_call_target="tpu_custom_call" | custom-call | tf_op jit(solution)/shard_map/pallas_call | solution.py:400
  51.3 51.0 %shard_map.87 = (f32[128,128]{1,0:T(8,128)}, f32[2,4,4,8,16,128]{5,4,3,2,1,0:T(8,128)}) custom-call(s32[1,16]{1,0:T(1,128)} %lens_ref.1, bf16[128,36864]{1,0:T(8,128)(2,1)} %bitcast.9, bf16[128,8192]{1,0:T(8,128)(2,1)} %bitcast.10, bf16[128,7168]{1,0:T(8,128)(2,1)} %bitcast.11, bf16[1280,576]{1,0:T(8,128)(2,1)} %get-tuple-element.7.lat_hbm, ...), custom_call_target="tpu_custom_call" | custom-call | flops 20000000000 | bytes 18000000 | tf_op jit(solution)/shard_map/pallas_call | solution.py:255
  102.3 1.5 %slice_reduce_fusion = f32[128]{0:T(128)} fusion(f32[128,128]{1,0:T(8,128)} %get-tuple-element.10), kind=kLoop, calls=%fused_computation | loop fusion | bytes 1024 | tf_op jit(solution)/shard_map/slice | solution.py:490
  103.8 34.0 %shard_map.88 = f32[28,64]{1,0:T(8,128)} custom-call(f32[2,4,4,8,16,128]{5,4,3,2,1,0:T(8,128)} %get-tuple-element.11.part_ref), custom_call_target="tpu_custom_call" | custom-call | tf_op jit(solution)/shard_map/pallas_call | solution.py:465
  137.8 1.3 copy.12

commit v2 on v0

v2 whole, which is shorter than its diff:
```python
import math

import jax
import jax.numpy as jnp
from jax import lax
from jax.experimental import pallas as pl
from jax.experimental.pallas import tpu as pltpu
from jax.sharding import Mesh
from jax.sharding import PartitionSpec as P

SEQ = ("seq_0", "seq_1", "seq_2")
SEQ_GRP = ("seq_0", "seq_1", "seq_2", "grp")
MESH = pl.DeviceIdType.MESH

ROWS = 128
HEADS = 64
LAT = 576
DI = 128
WIN = 1152
LOOK = 1024
D = 7168
DOCS = 16
PAIR = 2 * LAT
CUT = 640
DEEP = 768
PANEL = WIN + ROWS
QUARTER = D // 4
UNIT = 4 * ROWS
SLOTS = 4
NEG = -1e30
TARGET_SCALE = 0.07216878364870322
EXP_SCALE = TARGET_SCALE * math.log2(math.e)
BF = jnp.bfloat16
F32 = jnp.float32
VMEM_MOST = 67_043_328


def sync_with(peers):
    barrier = pltpu.get_barrier_semaphore()
    for peer in peers:
        pl.semaphore_signal(barrier, inc=1, device_id=peer, device_id_type=MESH)
    pl.semaphore_wait(barrier, len(peers))


def chip_after(y, z):
    return {"seq_0": lax.rem(y + (z + 1) // 8, 4), "seq_1": lax.rem(z + 1, 8)}


def chip_before(y, z):
    return {"seq_0": lax.rem(y + 3 + (z + 7) // 8, 4), "seq_1": lax.rem(z + 7, 8)}


def kernel(
    lens_ref, q_hbm, iq_hbm, hid_hbm, lat_hbm, ik_hbm, gw_ref,
    div_ref, out_ref,
    ke, ko, ikt, qbuf, rel_a, rel_b, acc, score, dif, starts, divs, gates, hid, lat, ik, gd,
    wx, wcat, wb, hy, ht, gall, part, rc, s1, rx, s2, rz, s3, fin,
    qsem, isem, ring_s, ring_r, side_s, side_r, w_s, w_r, t_s, t_r,
):
    y, z, core, x = (lax.axis_index(a) for a in SEQ_GRP)
    chip = y * 8 + z
    seq = chip * 2 + core
    window = pl.ds(pl.multiple_of(core * ROWS, ROWS), WIN)
    ahead, behind = chip_after(y, z), chip_before(y, z)
    partner = {"seq_2": 1 - core}
    xs = [{"grp": lax.rem(x + d, 4)} for d in range(1, 4)]
    ys = [{"seq_0": lax.rem(y + d, 4)} for d in range(1, 4)]
    zs = [{"seq_1": lax.rem(z + d, 8)} for d in range(1, 8)]

    def local(src, dst, sem):
        return pltpu.make_async_copy(src, dst, sem)

    def remote(src, dst, send, recv, peer):
        return pltpu.make_async_remote_copy(
            src_ref=src, dst_ref=dst, send_sem=send, recv_sem=recv, device_id=peer, device_id_type=MESH
        )

    def slot(k):
        return 8 - 2 * k + core

    def slot_rows(k):
        return pl.ds(pl.multiple_of((8 - 2 * k + core) * ROWS, ROWS), ROWS)

    def q_copy(unit, slot):
        quad, parity = unit // 2, unit % 2
        return [
            local(
                q_hbm.at[:, pl.ds(pl.multiple_of((quad * 4 + k) * PAIR + parity * (PAIR - CUT), 128), CUT)],
                qbuf.at[slot, pl.ds(k * ROWS, ROWS), pl.ds(0, CUT)],
                qsem.at[slot, k],
            )
            for k in range(4)
        ]

    own_lat = local(lat_hbm, lat.at[slot(0)], isem.at[0])
    own_ik = local(ik_hbm, ik.at[slot_rows(0)], isem.at[1])
    own_lat.start()
    own_ik.start()
    for u in range(SLOTS):
        for c in q_copy(u, u):
            c.start()
    sync_with([partner] + xs + ys + zs + [ahead, behind])

    def ring(k):
        src_lat, src_ik = (lat_hbm, ik_hbm) if k == 0 else (lat.at[slot(k)], ik.at[slot_rows(k)])
        return [
            remote(src_lat, lat.at[slot(k + 1)], ring_s.at[k, 0], ring_r.at[k, 0], ahead),
            remote(src_ik, ik.at[slot_rows(k + 1)], ring_s.at[k, 1], ring_r.at[k, 1], ahead),
        ]

    def side(k):
        src_lat, src_ik = (lat_hbm, ik_hbm) if k == 0 else (lat.at[slot(k)], ik.at[slot_rows(k)])
        return [
            remote(src_lat, lat.at[slot(k)], side_s.at[k, 0], side_r.at[k, 0], partner),
            remote(src_ik, ik.at[slot_rows(k)], side_s.at[k, 1], side_r.at[k, 1], partner),
        ]

    hop = ring(0)
    for c in hop:
        c.start()
    beside = side(0)
    for c in beside:
        c.start()
    wx[x] = gw_ref[...]
    w_copies = [remote(gw_ref, wx.at[x], w_s.at[d], w_r.at[d], xs[d - 1]) for d in range(1, 4)]
    for c in w_copies:
        c.start()
    hid_in = local(hid_hbm, hid, isem.at[3])
    own_quarter = local(hid_hbm.at[:, pl.ds(pl.multiple_of(y * QUARTER, 128), QUARTER)], hy.at[y], isem.at[4])
    hid_in.start()
    own_quarter.start()

    row = lax.broadcasted_iota(jnp.int32, (ROWS, ROWS), 0)
    lane = lax.broadcasted_iota(jnp.int32, (ROWS, ROWS), 1)
    pos = seq * ROWS + row
    start = jnp.zeros((ROWS, ROWS), jnp.int32)
    end = jnp.int32(0)
    for k in range(DOCS):
        length = lens_ref[0, k]
        end = end + length
        start = start + jnp.where(pos >= end, length, 0)
    starts[...] = start
    eye = jnp.where(row == lane, 1.0, 0.0).astype(BF)
    for u in range(SLOTS):
        for k in range(4):
            qbuf[u, k * ROWS : (k + 1) * ROWS, CUT:DEEP] = eye
    ke[LAT:CUT, :] = jnp.zeros((CUT - LAT, 2 * ROWS), BF)
    ko[0 : CUT - LAT, :] = jnp.zeros((CUT - LAT, 2 * ROWS), BF)
    acc[...] = jnp.zeros((ROWS, WIN), F32)
    score[...] = jnp.zeros((ROWS, WIN), F32)
    gd[...] = jnp.zeros((ROWS, ROWS), F32)
    gates[...] = jnp.zeros((ROWS, ROWS), F32)
    own_lat.wait()
    own_ik.wait()

    def keys_of(k):
        for j in range(2):
            at = (8 - 2 * k + j) * ROWS
            cols = slice(j * ROWS, (j + 1) * ROWS)
            key = (chip * 2 - 8 + 8 - 2 * k + j) * ROWS + lane
            own_start = starts[...]
            bias = jnp.where(jnp.logical_and(key >= own_start, key <= pos), 0.0, NEG).astype(BF)
            ke[CUT:DEEP, cols] = bias
            ko[CUT:DEEP, cols] = bias
            ke[0:LAT, cols] = lat[8 - 2 * k + j]
            ko[CUT - LAT : CUT, cols] = lat[8 - 2 * k + j]
            ikt[:, at : at + ROWS] = ik[at : at + ROWS, :].T

    for k in range(5):
        if k:
            for c in hop:
                c.wait()
            if k < 4:
                hop = ring(k)
                for c in hop:
                    c.start()
            beside = side(k)
            for c in beside:
                c.start()
        if k == 1:
            for c in w_copies:
                c.wait()
            for j in range(4):
                wcat[28 * j : 28 * j + 28, :] = wx[j].astype(F32)
            wb[y, z, core] = wcat[...].astype(BF)
            w_copies = [
                remote(wb.at[y, z, core], wb.at[y, z, core], w_s.at[3 + d], w_r.at[3 + d], zs[d - 1])
                for d in range(1, 8)
            ]
        if k == 2:
            for c in w_copies:
                c.wait()
            w_copies = [
                remote(wb.at[y, :, core], wb.at[y, :, core], w_s.at[10 + d], w_r.at[10 + d], ys[d - 1])
                for d in range(1, 4)
            ]
        if k == 4:
            for c in w_copies:
                c.wait()
            w_copies = [remote(wb.at[:, :, core], wb.at[:, :, core], w_s.at[0], w_r.at[0], partner)]
            h_copies = [
                remote(
                    hid_hbm.at[:, pl.ds(pl.multiple_of(lax.rem(y + d, 4) * QUARTER, 128), QUARTER)],
                    hy.at[y], w_s.at[13 + d], w_r.at[13 + d], ys[d - 1],
                )
                for d in range(1, 4)
            ]
        if k in (1, 2, 4):
            for c in w_copies:
                c.start()
        if k == 4:
            for c in h_copies:
                c.start()
        for c in beside:
            c.wait()
        keys_of(k)
        cols = slice((8 - 2 * k) * ROWS, (10 - 2 * k) * ROWS)

        def units(i, _, cols=cols, k=k):
            for parity, keys, store in ((0, ke, rel_a), (1, ko, rel_b)):
                unit = 2 * i + parity
                slot = unit % SLOTS
                for c in q_copy(unit, slot):
                    c.wait()
                store[i, :, cols] = jnp.dot(qbuf[slot], keys[...], preferred_element_type=F32)
                if k < 4:
                    for c in q_copy((unit + SLOTS) % 16, slot):
                        c.start()
                else:

                    @pl.when(unit + SLOTS < 16)
                    def _():
                        for c in q_copy(unit + SLOTS, slot):
                            c.start()

            return 0

        lax.fori_loop(0, 8, units, 0)

    iq_copies = [
        local(
            iq_hbm.at[:, pl.ds(u * 4 * DI, 4 * DI)],
            qbuf.at[u // 4, pl.ds(u % 4 * ROWS, ROWS), pl.ds(0, 4 * DI)],
            qsem.at[u // 4, u % 4],
        )
        for u in range(16)
    ]
    for c in iq_copies:
        c.start()
    for c in w_copies:
        c.wait()

    hid_in.wait()
    gates[:, 0:HEADS] = jnp.dot(hid[...], wb[...].reshape(D, HEADS), preferred_element_type=F32)
    for c in iq_copies:
        c.wait()

    def heads_sum(src):
        for g in range(ROWS // 8):
            rows = slice(8 * g, 8 * g + 8)
            total = acc[rows, :]
            for k in range(4):
                s = src[k * ROWS + 8 * g : k * ROWS + 8 * g + 8, window]
                top = jnp.max(s, axis=1, keepdims=True)
                p = jnp.exp2((s - top) * EXP_SCALE)
                total = total + p * (1.0 / jnp.sum(p, axis=1, keepdims=True))
            acc[rows, :] = total

    def relus(unit, dest):
        q4 = jnp.concatenate(
            [
                qbuf[unit // 4, pl.ds(pl.multiple_of(unit % 4 * ROWS, ROWS), ROWS), k * DI : (k + 1) * DI]
                for k in range(4)
            ],
            axis=0,
        )
        dest[:, 0:WIN] = jnp.dot(q4, ikt[:, window], preferred_element_type=F32)

    def score_sum(unit, src):
        mine = pltpu.roll(gates[...], lax.rem(ROWS - 4 * unit, ROWS), 1)
        for g in range(ROWS // 8):
            rows = slice(8 * g, 8 * g + 8)
            total = score[rows, :]
            for k in range(4):
                gate = mine[rows, k : k + 1]
                s = src[k * ROWS + 8 * g : k * ROWS + 8 * g + 8, 0:WIN]
                total = total + gate * jnp.maximum(s, 0.0)
            score[rows, :] = total

    heads_sum(rel_a.at[0])

    def mixed(i, last):
        relus(2 * i, rel_a.at[i])
        heads_sum(rel_b.at[i])
        relus(2 * i + 1, rel_b.at[i])
        score_sum(2 * i, rel_a.at[i])
        if not last:
            heads_sum(rel_a.at[i + 1])
        score_sum(2 * i + 1, rel_b.at[i])
        return 0

    lax.fori_loop(0, 7, lambda i, _: mixed(i, False), 0)
    mixed(7, True)

    factor = DI**-0.5
    key8 = seq * ROWS - LOOK + lax.broadcasted_iota(jnp.int32, (8, WIN), 1)
    row8 = seq * ROWS + lax.broadcasted_iota(jnp.int32, (8, WIN), 0)
    for g in range(ROWS // 8):
        rows = slice(8 * g, 8 * g + 8)
        start8 = jnp.concatenate([starts[rows, :]] * 9, axis=1)
        allowed = jnp.logical_and(key8 >= start8, key8 <= row8 + 8 * g)
        sc = jnp.where(allowed, score[rows, :] * factor, NEG)
        shifted = sc - jnp.max(sc, axis=1, keepdims=True)
        log_model = shifted - jnp.log(jnp.sum(jnp.exp(shifted), axis=1, keepdims=True))
        model = jnp.exp(log_model)
        target = acc[rows, :] * (1.0 / HEADS)
        positive = target > 0.0
        terms = jnp.where(positive, target * (jnp.log(jnp.where(positive, target, 1.0)) - log_model), 0.0)
        terms = jnp.where(allowed, terms, 0.0)
        divs[rows, :] = jnp.broadcast_to(jnp.sum(terms, axis=1, keepdims=True), (8, ROWS))
        dif[rows, :] = jnp.where(allowed, model - target, 0.0)
    div_ref[...] = divs[...].T[0:1, :]

    lane8 = lax.broadcasted_iota(jnp.int32, (8, ROWS), 1)

    def delta_sum(unit, src):
        for g in range(ROWS // 8):
            rows = slice(8 * g, 8 * g + 8)
            out = gd[rows, :]
            d8 = dif[rows, :]
            for k in range(4):
                s = src[k * ROWS + 8 * g : k * ROWS + 8 * g + 8, 0:WIN]
                value = jnp.sum(d8 * jnp.maximum(s, 0.0), axis=1, keepdims=True)
                out = jnp.where(lane8 == unit * 4 + k, value, out)
            gd[rows, :] = out

    def delta_step(i, _):
        delta_sum(2 * i, rel_a.at[i])
        delta_sum(2 * i + 1, rel_b.at[i])
        return 0

    lax.fori_loop(0, 8, delta_step, 0)
    delta = (gd[...] * factor / ROWS).astype(BF)
    gall[y] = delta
    g_copies = [remote(gall.at[y], gall.at[y], t_s.at[d], t_r.at[d], ys[d - 1]) for d in range(1, 4)]
    for c in g_copies:
        c.start()

    own_quarter.wait()
    for c in h_copies:
        c.wait()
    for j in range(4):
        for t in range(QUARTER // 128):
            ht[j, t * 128 : t * 128 + 128, :] = hy[j, :, t * 128 : t * 128 + 128].T
    for c in g_copies:
        c.wait()
    stack = []
    for j in range(4):
        wide = gall[j].astype(F32)
        stack += [wide, pltpu.roll(wide, 64, 1)]
    stack = jnp.concatenate(stack, axis=0).astype(BF)

    def part_step(i, _):
        lhs = jnp.concatenate(
            [
                ht[j, pl.ds(pl.multiple_of(i * 224 + c * 112, 16), 112), :]
                for j in range(4)
                for c in range(2)
            ],
            axis=1,
        )
        out = jnp.dot(lhs, stack, preferred_element_type=F32)
        pad = jnp.zeros((2, ROWS), F32)
        for xx in range(4):
            for half in range(2):
                at = xx * 28 + half * 14
                part[half, xx, i] = jnp.concatenate([out[at : at + 14, :], pad], axis=0)
        return 0

    lax.fori_loop(0, 8, part_step, 0)

    def exchange(copies):
        for c in copies:
            c.start()
        for c in copies:
            c.wait()

    exchange([remote(part.at[1 - core], rc, t_s.at[0], t_r.at[0], partner)])
    s1[...] = part[core] + rc[...]
    exchange([
        remote(s1.at[lax.rem(x + d, 4)], rx.at[d - 1], t_s.at[3 + d], t_r.at[3 + d], xs[d - 1])
        for d in range(1, 4)
    ])
    s2[...] = s1[x] + rx[0] + rx[1] + rx[2]
    exchange([
        remote(s2.at[lax.rem(z + d, 8)], rz.at[d - 1], t_s.at[6 + d], t_r.at[6 + d], zs[d - 1])
        for d in range(1, 8)
    ])
    total = s2[z]
    for d in range(7):
        total = total + rz[d]
    s3[...] = total
    exchange([remote(s3, fin, t_s.at[14], t_r.at[14], partner)])
    low = jnp.where(core == 0, s3[...], fin[...])
    high = jnp.where(core == 0, fin[...], s3[...])
    full = jnp.concatenate([low[0:14, :], high[0:14, :]], axis=0)
    out_ref[...] = jnp.where(core == 0, full[:, 0:64], full[:, 64:128])


def body(doc_lengths, hidden, gate_weight, target_query, latent_keys, index_query, index_keys):
    hbm = pl.BlockSpec(memory_space=pl.ANY)
    vmem = pl.BlockSpec(memory_space=pltpu.VMEM)
    dma = pltpu.SemaphoreType.DMA
    return pl.pallas_call(
        kernel,
        out_shape=(jax.ShapeDtypeStruct((1, ROWS), F32), jax.ShapeDtypeStruct((28, HEADS), F32)),
        in_specs=[pl.BlockSpec(memory_space=pltpu.SMEM)] + [hbm] * 5 + [vmem],
        out_specs=(vmem, vmem),
        scratch_shapes=[
            pltpu.VMEM((DEEP, 2 * ROWS), BF),
            pltpu.VMEM((DEEP, 2 * ROWS), BF),
            pltpu.VMEM((DI, PANEL), BF),
            pltpu.VMEM((SLOTS, UNIT, DEEP), BF),
            pltpu.VMEM((8, UNIT, PANEL), F32),
            pltpu.VMEM((8, UNIT, PANEL), F32),
            pltpu.VMEM((ROWS, WIN), F32),
            pltpu.VMEM((ROWS, WIN), F32),
            pltpu.VMEM((ROWS, WIN), F32),
            pltpu.VMEM((ROWS, ROWS), jnp.int32),
            pltpu.VMEM((ROWS, ROWS), F32),
            pltpu.VMEM((ROWS, ROWS), F32),
            pltpu.VMEM((ROWS, D), BF),
            pltpu.VMEM((10, LAT, ROWS), BF),
            pltpu.VMEM((PANEL, DI), BF),
            pltpu.VMEM((ROWS, ROWS), F32),
            pltpu.VMEM((4, 28, HEADS), BF),
            pltpu.VMEM((112, HEADS), F32),
            pltpu.VMEM((4, 8, 2, 112, HEADS), BF),
            pltpu.VMEM((4, ROWS, QUARTER), BF),
            pltpu.VMEM((4, QUARTER, ROWS), BF),
            pltpu.VMEM((4, ROWS, ROWS), BF),
            pltpu.VMEM((2, 4, 8, 16, ROWS), F32),
            pltpu.VMEM((4, 8, 16, ROWS), F32),
            pltpu.VMEM((4, 8, 16, ROWS), F32),
            pltpu.VMEM((3, 8, 16, ROWS), F32),
            pltpu.VMEM((8, 16, ROWS), F32),
            pltpu.VMEM((7, 16, ROWS), F32),
            pltpu.VMEM((16, ROWS), F32),
            pltpu.VMEM((16, ROWS), F32),
            dma((SLOTS, 4)), dma((5,)),
            dma((4, 2)), dma((4, 2)), dma((5, 2)), dma((5, 2)),
            dma((17,)), dma((17,)), dma((15,)), dma((15,)),
        ],
        compiler_params=pltpu.CompilerParams(
            collective_id=0, has_side_effects=True, vmem_limit_bytes=VMEM_MOST
        ),
    )(doc_lengths, target_query[0], index_query[0], hidden[0], latent_keys[0].T, index_keys[0], gate_weight)


def solution(mesh):
    split = Mesh(mesh.devices.reshape(4, 8, 2, mesh.shape["grp"]), SEQ_GRP)
    rows = P("grp", SEQ, None)
    in_specs = (P("grp", None), rows, P(SEQ_GRP, None), rows, rows, rows, rows)
    out_specs = (P("grp", SEQ), P(SEQ_GRP, None))
    return jax.shard_map(body, mesh=split, in_specs=in_specs, out_specs=out_specs, check_vma=False)
```

time: 1320 us -> 111 us (0.08)
  the two profiles are of different devices: /device:TPU:8 before, /device:TPU:1 now
where the time goes in v2:
time: 111 us
  Pallas kernels  108 us (97%)
  local copies, waits for them, and re-layouts  2.46 us (2%)
    pallas_call x1, Pallas kernels, body(): pl.pallas_call(kernel, out_shape=(jax.ShapeDtypeStruct((1, ROWS), F32), j...  108 us
    unnamed x2, local copies, waits for them, and re-layouts  2.46 us

profile of v2, /device:TPU:1, one launch (start us, length us, event | category | flops | bytes accessed | tf_op | source)
XLA Modules:
  0.0 111.0 jit_solution(13319183149558055948)
XLA Ops:
  0.6 107.9 %shard_map.86 = (f32[1,128]{1,0:T(1,128)}, f32[28,64]{1,0:T(8,128)}) custom-call(s32[1,16]{1,0:T(1,128)} %lens_ref.1, bf16[128,36864]{1,0:T(8,128)(2,1)} %bitcast.7, bf16[128,8192]{1,0:T(8,128)(2,1)} %bitcast.8, bf16[128,7168]{1,0:T(8,128)(2,1)} %bitcast.9, bf16[576,128]{1,0:T(8,128)(2,1)} %bitcast.10, bf16[128,128]{1,0:T(8,128)(2,1)} %bitcast.11, ...), custom_call_target="tpu_custom_call" | custom-call | tf_op jit(solution)/shard_map/pallas_call | solution.py:414
  108.6 1.1 %copy.11 = f32[1,128]{1,0:T(1,128)} copy(f32[1,128]{1,0:T(1,128)} %get-tuple-element.4) | data formatting | bytes 1024
  109.7 1.3 %copy.12 = f32[28,64]{1,0:T(8,128)} copy(f32[28,64]{1,0:T(8,128)} %get-tuple-element.5) | data formatting | bytes 14336

commit v3 on v2

--- a/solution.py
+++ b/solution.py
@@ -26,7 +26,8 @@
 PANEL = WIN + ROWS
 QUARTER = D // 4
 UNIT = 4 * ROWS
-SLOTS = 4
+PASSES = ((6, 3), (2, 4), (0, 2))
+SLOTS = 8
 NEG = -1e30
 TARGET_SCALE = 0.07216878364870322
 EXP_SCALE = TARGET_SCALE * math.log2(math.e)
@@ -60,7 +61,6 @@
     y, z, core, x = (lax.axis_index(a) for a in SEQ_GRP)
     chip = y * 8 + z
     seq = chip * 2 + core
-    window = pl.ds(pl.multiple_of(core * ROWS, ROWS), WIN)
     ahead, behind = chip_after(y, z), chip_before(y, z)
     partner = {"seq_2": 1 - core}
     xs = [{"grp": lax.rem(x + d, 4)} for d in range(1, 4)]
@@ -87,10 +87,14 @@
             local(
                 q_hbm.at[:, pl.ds(pl.multiple_of((quad * 4 + k) * PAIR + parity * (PAIR - CUT), 128), CUT)],
                 qbuf.at[slot, pl.ds(k * ROWS, ROWS), pl.ds(0, CUT)],
-                qsem.at[slot, k],
+                qsem.at[slot],
             )
             for k in range(4)
         ]
+
+    def q_wait(slot):
+        whole = qbuf.at[slot, :, pl.ds(0, CUT)]
+        local(whole, whole, qsem.at[slot]).wait()
 
     own_lat = local(lat_hbm, lat.at[slot(0)], isem.at[0])
     own_ik = local(ik_hbm, ik.at[slot_rows(0)], isem.at[1])
@@ -101,26 +105,43 @@
             c.start()
     sync_with([partner] + xs + ys + zs + [ahead, behind])
 
-    def ring(k):
-        src_lat, src_ik = (lat_hbm, ik_hbm) if k == 0 else (lat.at[slot(k)], ik.at[slot_rows(k)])
+    def halves(k, own):
+        lat_at, ik_at = (lat_hbm, ik_hbm) if own else (lat.at[slot(k)], ik.at[slot_rows(k)])
+        half = LAT // 2
+        return [[lat_at.at[pl.ds(0, half)]], [lat_at.at[pl.ds(half, half)], ik_at]]
+
+    def ring(k, part):
         return [
-            remote(src_lat, lat.at[slot(k + 1)], ring_s.at[k, 0], ring_r.at[k, 0], ahead),
-            remote(src_ik, ik.at[slot_rows(k + 1)], ring_s.at[k, 1], ring_r.at[k, 1], ahead),
+            remote(a, b, ring_s.at[k, part + n], ring_r.at[k, part + n], ahead)
+            for n, (a, b) in enumerate(zip(halves(k, k == 0)[part], halves(k + 1, False)[part]))
         ]
 
-    def side(k):
-        src_lat, src_ik = (lat_hbm, ik_hbm) if k == 0 else (lat.at[slot(k)], ik.at[slot_rows(k)])
+    def side(k, part):
         return [
-            remote(src_lat, lat.at[slot(k)], side_s.at[k, 0], side_r.at[k, 0], partner),
-            remote(src_ik, ik.at[slot_rows(k)], side_s.at[k, 1], side_r.at[k, 1], partner),
+            remote(a, b, side_s.at[k, part + n], side_r.at[k, part + n], partner)
+            for n, (a, b) in enumerate(zip(halves(k, k == 0)[part], halves(k, False)[part]))
         ]
 
-    hop = ring(0)
-    for c in hop:
-        c.start()
-    beside = side(0)
-    for c in beside:
-        c.start()
+    hops = {}
+    besides = []
+
+    def start_from(k, part):
+        if k < 4:
+            hops[k + 1, part] = ring(k, part)
+            for c in hops[k + 1, part]:
+                c.start()
+        pair = side(k, part)
+        for c in pair:
+            c.start()
+        besides.extend(pair)
+
+    def arrive(k, part):
+        for c in hops[k, part]:
+            c.wait()
+        start_from(k, part)
+
+    start_from(0, 0)
+    start_from(0, 1)
     wx[x] = gw_ref[...]
     w_copies = [remote(gw_ref, wx.at[x], w_s.at[d], w_r.at[d], xs[d - 1]) for d in range(1, 4)]
     for c in w_copies:
@@ -144,8 +165,8 @@
     for u in range(SLOTS):
         for k in range(4):
             qbuf[u, k * ROWS : (k + 1) * ROWS, CUT:DEEP] = eye
-    ke[LAT:CUT, :] = jnp.zeros((CUT - LAT, 2 * ROWS), BF)
-    ko[0 : CUT - LAT, :] = jnp.zeros((CUT - LAT, 2 * ROWS), BF)
+    ke[LAT:CUT, :] = jnp.zeros((CUT - LAT, 4 * ROWS), BF)
+    ko[0 : CUT - LAT, :] = jnp.zeros((CUT - LAT, 4 * ROWS), BF)
     acc[...] = jnp.zeros((ROWS, WIN), F32)
     score[...] = jnp.zeros((ROWS, WIN), F32)
     gd[...] = jnp.zeros((ROWS, ROWS), F32)
@@ -153,31 +174,49 @@
     own_lat.wait()
     own_ik.wait()
 
-    def keys_of(k):
-        for j in range(2):
-            at = (8 - 2 * k + j) * ROWS
+    def keys_of(first, count):
+        for j in range(count):
+            at = (first + j) * ROWS
             cols = slice(j * ROWS, (j + 1) * ROWS)
-            key = (chip * 2 - 8 + 8 - 2 * k + j) * ROWS + lane
+            key = seq * ROWS - LOOK + at + lane
             own_start = starts[...]
             bias = jnp.where(jnp.logical_and(key >= own_start, key <= pos), 0.0, NEG).astype(BF)
             ke[CUT:DEEP, cols] = bias
             ko[CUT:DEEP, cols] = bias
-            ke[0:LAT, cols] = lat[8 - 2 * k + j]
-            ko[CUT - LAT : CUT, cols] = lat[8 - 2 * k + j]
-            ikt[:, at : at + ROWS] = ik[at : at + ROWS, :].T
-
-    for k in range(5):
-        if k:
-            for c in hop:
-                c.wait()
-            if k < 4:
-                hop = ring(k)
-                for c in hop:
-                    c.start()
-            beside = side(k)
-            for c in beside:
-                c.start()
-        if k == 1:
+            block = lat[core + first + j]
+            ke[0:LAT, cols] = block
+            ko[CUT - LAT : CUT, cols] = block
+            rows = pl.ds(pl.multiple_of((core + first + j) * ROWS, ROWS), ROWS)
+            ikt[:, at : at + ROWS] = ik[rows, :].T
+
+    def some_units(lo, hi, first, count, last):
+        def units(i, _):
+            for parity, keys, store in ((0, ke, rel_a), (1, ko, rel_b)):
+                unit = 2 * i + parity
+                slot = lax.rem(unit, SLOTS)
+                q_wait(slot)
+                store[i, :, first * ROWS : (first + count) * ROWS] = jnp.dot(
+                    qbuf[slot], keys[:, 0 : count * ROWS], preferred_element_type=F32
+                )
+                if not last:
+                    for c in q_copy(lax.rem(unit + SLOTS, 16), slot):
+                        c.start()
+                else:
+
+                    @pl.when(unit + SLOTS < 16)
+                    def _():
+                        for c in q_copy(unit + SLOTS, slot):
+                            c.start()
+
+            return 0
+
+        lax.fori_loop(lo, hi, units, 0)
+
+    parts = [(k, part) for k in range(1, 5) for part in range(2)]
+    for n, (first, count) in enumerate(PASSES):
+        while parts and parts[0][0] <= (9 - first) // 2:
+            arrive(*parts.pop(0))
+        if n == 0:
             for c in w_copies:
                 c.wait()
             for j in range(4):
@@ -187,17 +226,13 @@
                 remote(wb.at[y, z, core], wb.at[y, z, core], w_s.at[3 + d], w_r.at[3 + d], zs[d - 1])
                 for d in range(1, 8)
             ]
-        if k == 2:
+        if n == 1:
             for c in w_copies:
                 c.wait()
             w_copies = [
                 remote(wb.at[y, :, core], wb.at[y, :, core], w_s.at[10 + d], w_r.at[10 + d], ys[d - 1])
                 for d in range(1, 4)
             ]
-        if k == 4:
-            for c in w_copies:
-                c.wait()
-            w_copies = [remote(wb.at[:, :, core], wb.at[:, :, core], w_s.at[0], w_r.at[0], partner)]
             h_copies = [
                 remote(
                     hid_hbm.at[:, pl.ds(pl.multiple_of(lax.rem(y + d, 4) * QUARTER, 128), QUARTER)],
@@ -205,43 +240,29 @@
                 )
                 for d in range(1, 4)
             ]
-        if k in (1, 2, 4):
+        if n == 2:
             for c in w_copies:
-                c.start()
-        if k == 4:
+                c.wait()
+            w_copies = [remote(wb.at[:, :, core], wb.at[:, :, core], w_s.at[0], w_r.at[0], partner)]
+        for c in w_copies:
+            c.start()
+        if n == 1:
             for c in h_copies:
                 c.start()
-        for c in beside:
+        for c in besides:
             c.wait()
-        keys_of(k)
-        cols = slice((8 - 2 * k) * ROWS, (10 - 2 * k) * ROWS)
-
-        def units(i, _, cols=cols, k=k):
-            for parity, keys, store in ((0, ke, rel_a), (1, ko, rel_b)):
-                unit = 2 * i + parity
-                slot = unit % SLOTS
-                for c in q_copy(unit, slot):
-                    c.wait()
-                store[i, :, cols] = jnp.dot(qbuf[slot], keys[...], preferred_element_type=F32)
-                if k < 4:
-                    for c in q_copy((unit + SLOTS) % 16, slot):
-                        c.start()
-                else:
-
-                    @pl.when(unit + SLOTS < 16)
-                    def _():
-                        for c in q_copy(unit + SLOTS, slot):
-                            c.start()
-
-            return 0
-
-        lax.fori_loop(0, 8, units, 0)
+        besides.clear()
+        keys_of(first, count)
+        for quarter in range(4):
+            some_units(2 * quarter, 2 * quarter + 2, first, count, n == len(PASSES) - 1)
+            if quarter and parts:
+                arrive(*parts.pop(0))
 
     iq_copies = [
         local(
             iq_hbm.at[:, pl.ds(u * 4 * DI, 4 * DI)],
             qbuf.at[u // 4, pl.ds(u % 4 * ROWS, ROWS), pl.ds(0, 4 * DI)],
-            qsem.at[u // 4, u % 4],
+            isem.at[5 + u],
         )
         for u in range(16)
     ]
@@ -260,7 +281,7 @@
             rows = slice(8 * g, 8 * g + 8)
             total = acc[rows, :]
             for k in range(4):
-                s = src[k * ROWS + 8 * g : k * ROWS + 8 * g + 8, window]
+                s = src[k * ROWS + 8 * g : k * ROWS + 8 * g + 8, :]
                 top = jnp.max(s, axis=1, keepdims=True)
                 p = jnp.exp2((s - top) * EXP_SCALE)
                 total = total + p * (1.0 / jnp.sum(p, axis=1, keepdims=True))
@@ -274,7 +295,7 @@
             ],
             axis=0,
         )
-        dest[:, 0:WIN] = jnp.dot(q4, ikt[:, window], preferred_element_type=F32)
+        dest[...] = jnp.maximum(jnp.dot(q4, ikt[...], preferred_element_type=F32), 0.0)
 
     def score_sum(unit, src):
         mine = pltpu.roll(gates[...], lax.rem(ROWS - 4 * unit, ROWS), 1)
@@ -283,8 +304,8 @@
             total = score[rows, :]
             for k in range(4):
                 gate = mine[rows, k : k + 1]
-                s = src[k * ROWS + 8 * g : k * ROWS + 8 * g + 8, 0:WIN]
-                total = total + gate * jnp.maximum(s, 0.0)
+                s = src[k * ROWS + 8 * g : k * ROWS + 8 * g + 8, :]
+                total = total + gate * s
             score[rows, :] = total
 
     heads_sum(rel_a.at[0])
@@ -329,8 +350,8 @@
             out = gd[rows, :]
             d8 = dif[rows, :]
             for k in range(4):
-                s = src[k * ROWS + 8 * g : k * ROWS + 8 * g + 8, 0:WIN]
-                value = jnp.sum(d8 * jnp.maximum(s, 0.0), axis=1, keepdims=True)
+                s = src[k * ROWS + 8 * g : k * ROWS + 8 * g + 8, :]
+                value = jnp.sum(d8 * s, axis=1, keepdims=True)
                 out = jnp.where(lane8 == unit * 4 + k, value, out)
             gd[rows, :] = out
 
@@ -417,12 +438,12 @@
         in_specs=[pl.BlockSpec(memory_space=pltpu.SMEM)] + [hbm] * 5 + [vmem],
         out_specs=(vmem, vmem),
         scratch_shapes=[
-            pltpu.VMEM((DEEP, 2 * ROWS), BF),
-            pltpu.VMEM((DEEP, 2 * ROWS), BF),
-            pltpu.VMEM((DI, PANEL), BF),
+            pltpu.VMEM((DEEP, 4 * ROWS), BF),
+            pltpu.VMEM((DEEP, 4 * ROWS), BF),
+            pltpu.VMEM((DI, WIN), BF),
             pltpu.VMEM((SLOTS, UNIT, DEEP), BF),
-            pltpu.VMEM((8, UNIT, PANEL), F32),
-            pltpu.VMEM((8, UNIT, PANEL), F32),
+            pltpu.VMEM((8, UNIT, WIN), F32),
+            pltpu.VMEM((8, UNIT, WIN), F32),
             pltpu.VMEM((ROWS, WIN), F32),
             pltpu.VMEM((ROWS, WIN), F32),
             pltpu.VMEM((ROWS, WIN), F32),
@@ -447,8 +468,8 @@
             pltpu.VMEM((7, 16, ROWS), F32),
             pltpu.VMEM((16, ROWS), F32),
             pltpu.VMEM((16, ROWS), F32),
-            dma((SLOTS, 4)), dma((5,)),
-            dma((4, 2)), dma((4, 2)), dma((5, 2)), dma((5, 2)),
+            dma((SLOTS,)), dma((21,)),
+            dma((4, 3)), dma((4, 3)), dma((5, 3)), dma((5, 3)),
             dma((17,)), dma((17,)), dma((15,)), dma((15,)),
         ],
         compiler_params=pltpu.CompilerParams(

time: 111 us -> 100 us (0.901)
  Pallas kernels: 108 us -> 96.7 us
    pallas_call x1, Pallas kernels: 108 us -> 96.7 us  [body(): pl.pallas_call(kernel, out_shape=(jax.ShapeDtypeStruct((1, ROWS), F32), j...]
where the time goes in v3:
time: 100 us; the launch traced here: 99.8 us
  Pallas kernels  96.7 us (97%)
  local copies, waits for them, and re-layouts  2.46 us (2%)
    pallas_call x1, Pallas kernels, body(): pl.pallas_call(kernel, out_shape=(jax.ShapeDtypeStruct((1, ROWS), F32), j...  96.7 us
    unnamed x2, local copies, waits for them, and re-layouts  2.46 us

profile of v3, /device:TPU:1, one launch (start us, length us, event | category | flops | bytes accessed | tf_op | source)
XLA Modules:
  0.0 99.8 jit_solution(268248308510503035)
XLA Ops:
  0.6 96.7 %shard_map.86 = (f32[1,128]{1,0:T(1,128)}, f32[28,64]{1,0:T(8,128)}) custom-call(s32[1,16]{1,0:T(1,128)} %lens_ref.1, bf16[128,36864]{1,0:T(8,128)(2,1)} %bitcast.7, bf16[128,8192]{1,0:T(8,128)(2,1)} %bitcast.8, bf16[128,7168]{1,0:T(8,128)(2,1)} %bitcast.9, bf16[576,128]{1,0:T(8,128)(2,1)} %bitcast.10, bf16[128,128]{1,0:T(8,128)(2,1)} %bitcast.11, ...), custom_call_target="tpu_custom_call" | custom-call | tf_op jit(solution)/shard_map/pallas_call | solution.py:435
  97.4 1.1 %copy.11 = f32[1,128]{1,0:T(1,128)} copy(f32[1,128]{1,0:T(1,128)} %get-tuple-element.4) | data formatting | bytes 1024
  98.5 1.3 %copy.12 = f32[28,64]{1,0:T(8,128)} copy(f32[28,64]{1,0:T(8,128)} %get-tuple-element.5) | data formatting | bytes 14336
